TPU v7x, 32 devices: a whole 2x2x4 slice. The times are simulated.
32 devices in a mesh: dp: 8 (over y, x, core), context: 4 (over z).
Axes of the slice: x: 2, y: 2, z: 4, core: 2. Of those that a mesh axis runs over, the one named last changes fastest.
Arguments:
- image_tokens: bfloat16 [8, 448, 3072], P('dp', 'context'), may hold values from -6 to 6
- text_tokens: bfloat16 [8, 64, 3072], P('dp', 'context'), may hold values from -6 to 6
- image_mod: bfloat16 [8, 3, 3072], P('dp'), may hold values from -4 to 4
- text_mod: bfloat16 [8, 3, 3072], P('dp'), may hold values from -4 to 4
- image_qkv_weight: bfloat16 [3072, 3, 16, 128], P('dp', None, 'context'), may hold values from -0.109375 to 0.109375
- text_qkv_weight: bfloat16 [3072, 3, 16, 128], P('dp', None, 'context'), may hold values from -0.109375 to 0.109375
- image_out_weight: bfloat16 [3072, 16, 128], P('dp', 'context'), may hold values from -1 to 1
- text_out_weight: bfloat16 [3072, 16, 128], P('dp', 'context'), may hold values from -1 to 1
- image_slope: bfloat16 [8, 448, 3072], P('dp', 'context'), may hold values from -0.119628906 to 0.119628906
- text_slope: bfloat16 [8, 64, 3072], P('dp', 'context'), may hold values from -0.119628906 to 0.119628906
Outputs:
- image_update: bfloat16 [8, 448, 3072], P('dp', 'context')
- text_update: bfloat16 [8, 64, 3072], P('dp', 'context')
- image_qkv_grad: float32 [3072, 3, 16, 128], P('dp', None, 'context')
- text_qkv_grad: float32 [3072, 3, 16, 128], P('dp', None, 'context')
- image_out_grad: float32 [3072, 16, 128], P('dp', 'context')
- text_out_grad: float32 [3072, 16, 128], P('dp', 'context')
- image_mod_grad: float32 [8, 3, 3072], P('dp')
- text_mod_grad: float32 [8, 3, 3072], P('dp')
All inputs are finite; a program needn't handle non-finite values.
Results may differ from a plain program's by a relative error of at most 0.015.
Values may be sent and summed in bfloat16 or wider, within the bound.
No kernel may reach another device: no remote copies, remote signals or barrier semaphores. Data moves between devices by JAX's collectives and lax.ppermute only.
A program may use at most 128 MiB of HBM per device.

v0:
```python
import jax
import jax.numpy as jnp
from jax import lax
from jax.sharding import PartitionSpec as P

norm_eps = 1e-06


def layer_normal(values):
    average = jnp.mean(values, axis=-1, keepdims=True)
    centred = values - average
    return centred * lax.rsqrt(jnp.mean(centred * centred, axis=-1, keepdims=True) + norm_eps)


def rms_normal(values):
    factor = lax.rsqrt(jnp.mean(values * values, axis=-1, keepdims=True) + norm_eps)
    return (values * factor, factor)


def rms_back(normed, factor, slopes):
    return factor * (slopes - normed * jnp.mean(slopes * normed, axis=-1, keepdims=True))


def modulate(tokens, modulation):
    normal = layer_normal(tokens.astype(jnp.float32))
    factors = modulation.astype(jnp.float32)
    return (normal, ((1.0 + factors[1]) * normal + factors[0]).astype(jnp.bfloat16))


def contract_rows(left_side, right_side):
    return lax.dot_general(
        left_side, right_side, (((0,), (0,)), ((), ())), preferred_element_type=jnp.float32
    )


def contract_last(left_side, right_side):
    return lax.dot_general(
        left_side, right_side, (((1,), (1,)), ((), ())), preferred_element_type=jnp.float32
    )


def body(
    image_tokens,
    text_tokens,
    image_mod,
    text_mod,
    image_qkv_weight,
    text_qkv_weight,
    image_out_weight,
    text_out_weight,
    image_slope,
    text_slope,
):
    groups = lax.axis_size("context")
    own_image = image_tokens.shape[1]
    own_text = text_tokens.shape[1]
    block_rows = own_image + own_text
    model_width = image_tokens.shape[2]
    shard_rows = image_qkv_weight.shape[0]
    head_count = image_qkv_weight.shape[2]
    head_size = image_qkv_weight.shape[3]
    inner_width = head_count * head_size
    triple = 3 * inner_width
    text_rows = own_text * groups
    score_scale = head_size ** (-0.5)
    whole_image, whole_text, slopes_image, slopes_text = (
        lax.all_gather(image_tokens, "context", axis=1, tiled=True),
        lax.all_gather(text_tokens, "context", axis=1, tiled=True),
        lax.all_gather(image_slope, "context", axis=1, tiled=True),
        lax.all_gather(text_slope, "context", axis=1, tiled=True),
    )
    full_q_image, full_q_text, full_o_image, full_o_text = (
        lax.all_gather(image_qkv_weight, "dp", axis=0, tiled=True),
        lax.all_gather(text_qkv_weight, "dp", axis=0, tiled=True),
        lax.all_gather(image_out_weight, "dp", axis=0, tiled=True),
        lax.all_gather(text_out_weight, "dp", axis=0, tiled=True),
    )
    wq_image = full_q_image.reshape(model_width, triple)
    wq_text = full_q_text.reshape(model_width, triple)
    wo_image = full_o_image.reshape(model_width, inner_width)
    wo_text = full_o_text.reshape(model_width, inner_width)
    normal_image, input_image = modulate(whole_image[0], image_mod[0])
    normal_text, input_text = modulate(whole_text[0], text_mod[0])
    projected = jnp.concatenate(
        [
            jnp.dot(input_text, wq_text, preferred_element_type=jnp.float32),
            jnp.dot(input_image, wq_image, preferred_element_type=jnp.float32),
        ],
        axis=0,
    )
    projected = projected.reshape(-1, 3, head_count, head_size)
    query_normal, query_factor = rms_normal(projected[:, 0])
    key_normal, key_factor = rms_normal(projected[:, 1])
    query_b = query_normal.astype(jnp.bfloat16)
    key_b = key_normal.astype(jnp.bfloat16)
    value_b = projected[:, 2].astype(jnp.bfloat16)
    scores = (
        jnp.einsum("ihe,jhe->hij", query_b, key_b, preferred_element_type=jnp.float32) * score_scale
    )
    raised = jnp.exp(scores)
    attn_probs = raised / jnp.sum(raised, axis=-1, keepdims=True)
    probs_b = attn_probs.astype(jnp.bfloat16)
    attended = jnp.einsum(
        "hij,jhe->ihe", probs_b, value_b, preferred_element_type=jnp.float32
    ).astype(jnp.bfloat16)
    flat_att = attended.reshape(-1, inner_width)
    att_text = flat_att[:text_rows]
    att_image = flat_att[text_rows:]
    blocks_text = att_text.reshape(groups, own_text, inner_width)
    blocks_image = att_image.reshape(groups, own_image, inner_width)
    block_count = block_rows * lax.axis_size("context") // block_rows
    part_text = blocks_text.reshape(block_count * own_text, inner_width)
    part_image = blocks_image.reshape(block_count * own_image, inner_width)
    out_text = contract_last(part_text, wo_text).reshape(block_count, own_text, model_width)
    out_image = contract_last(part_image, wo_image).reshape(block_count, own_image, model_width)
    mixed_rows = lax.psum_scatter(
        jnp.concatenate([out_text, out_image], axis=1)
        .reshape(block_rows * lax.axis_size("context"), model_width)
        .astype(jnp.bfloat16),
        "context",
        scatter_dimension=0,
        tiled=True,
    ).astype(jnp.float32)
    mixed_text = mixed_rows[:own_text]
    mixed_image = mixed_rows[own_text:]
    factors_image = image_mod[0].astype(jnp.float32)
    factors_text = text_mod[0].astype(jnp.float32)
    update_image = (factors_image[2] * mixed_image).astype(jnp.bfloat16)[None]
    update_text = (factors_text[2] * mixed_text).astype(jnp.bfloat16)[None]
    gate_part_image = jnp.sum(image_slope[0].astype(jnp.float32) * mixed_image, axis=0)
    gate_part_text = jnp.sum(text_slope[0].astype(jnp.float32) * mixed_text, axis=0)
    gated_image = (factors_image[2] * slopes_image[0].astype(jnp.float32)).astype(jnp.bfloat16)
    gated_text = (factors_text[2] * slopes_text[0].astype(jnp.float32)).astype(jnp.bfloat16)
    back_att = jnp.concatenate(
        [
            jnp.dot(gated_text, wo_text, preferred_element_type=jnp.float32),
            jnp.dot(gated_image, wo_image, preferred_element_type=jnp.float32),
        ],
        axis=0,
    )
    back_att = back_att.astype(jnp.bfloat16).reshape(-1, head_count, head_size)
    back_probs = jnp.einsum("ihe,jhe->hij", back_att, value_b, preferred_element_type=jnp.float32)
    back_value = jnp.einsum("hij,ihe->jhe", probs_b, back_att, preferred_element_type=jnp.float32)
    back_scores = (
        attn_probs
        * (back_probs - jnp.sum(attn_probs * back_probs, axis=-1, keepdims=True))
        * score_scale
    ).astype(jnp.bfloat16)
    back_query = jnp.einsum("hij,jhe->ihe", back_scores, key_b, preferred_element_type=jnp.float32)
    back_key = jnp.einsum("hij,ihe->jhe", back_scores, query_b, preferred_element_type=jnp.float32)
    back_qkv = (
        jnp.stack(
            [
                rms_back(query_normal, query_factor, back_query),
                rms_back(key_normal, key_factor, back_key),
                back_value,
            ],
            axis=1,
        )
        .reshape(-1, triple)
        .astype(jnp.bfloat16)
    )
    back_text = back_qkv[:text_rows]
    back_image = back_qkv[text_rows:]
    spread_image = contract_last(back_image, wq_image)
    spread_text = contract_last(back_text, wq_text)
    part_image = jnp.stack(
        [
            jnp.sum(spread_image, axis=0),
            jnp.sum(spread_image * normal_image, axis=0),
            gate_part_image,
        ]
    )
    part_text = jnp.stack(
        [jnp.sum(spread_text, axis=0), jnp.sum(spread_text * normal_text, axis=0), gate_part_text]
    )
    modsum_image, modsum_text = (
        lax.psum(part_image.astype(jnp.bfloat16), "context").astype(jnp.float32),
        lax.psum(part_text.astype(jnp.bfloat16), "context").astype(jnp.float32),
    )
    pieces = [contract_rows(input_image, back_image)]
    pieces.append(contract_rows(gated_image, att_image))
    pieces.append(contract_rows(gated_text, att_text))
    summed = lax.psum_scatter(
        jnp.concatenate(pieces, axis=1).astype(jnp.bfloat16), "dp", scatter_dimension=0, tiled=True
    ).astype(jnp.float32)
    grad_q_image = summed[:, :triple]
    remaining = summed[:, triple:]
    columns = lax.all_to_all(input_text[None], "dp", split_axis=2, concat_axis=0, tiled=True)
    slopes_all = lax.all_gather(back_text[None], "dp", axis=0, tiled=True)
    per_image = jnp.einsum("itd,itj->idj", columns, slopes_all, preferred_element_type=jnp.float32)
    rounded = lax.optimization_barrier(per_image.astype(jnp.bfloat16))
    grad_q_text = jnp.sum(rounded.astype(jnp.float32), axis=0)
    grad_o_image = remaining[:, :inner_width]
    grad_o_text = remaining[:, inner_width:]
    return (
        update_image,
        update_text,
        grad_q_image.reshape(shard_rows, 3, head_count, head_size),
        grad_q_text.reshape(shard_rows, 3, head_count, head_size),
        grad_o_image.reshape(shard_rows, head_count, head_size),
        grad_o_text.reshape(shard_rows, head_count, head_size),
        modsum_image[None],
        modsum_text[None],
    )


def solution(mesh):
    placed = (
        P("dp", "context", None),
        P("dp", "context", None),
        P("dp", None, None),
        P("dp", None, None),
        P("dp", None, "context", None),
        P("dp", None, "context", None),
        P("dp", "context", None),
        P("dp", "context", None),
        P("dp", "context", None),
        P("dp", "context", None),
    )
    return jax.shard_map(
        body,
        mesh=mesh,
        in_specs=placed,
        out_specs=(
            P("dp", "context", None),
            P("dp", "context", None),
            P("dp", None, "context", None),
            P("dp", None, "context", None),
            P("dp", "context", None),
            P("dp", "context", None),
            P("dp", None, None),
            P("dp", None, None),
        ),
        check_vma=False,
    )
```

profile of v0, /device:TPU:0, one launch (start us, length us, event | category | flops | bytes accessed | tf_op | source)
XLA Modules:
  0.0 606.1 jit_solution(18341433870807146927)
XLA Ops:
  11.3 19.2 %all_gather.27 = bf16[1,64,3072]{2,1,0:T(8,128)(2,1)S(1)} all-gather(bf16[1,16,3072]{2,1,0:T(8,128)(2,1)S(1)} %copy-done.28), channel_id=1, replica_groups=mesh['dp'=8,'context'=4] {'context'}, dimensions={1}, use_global_device_ids=true | all-gather | bytes 491520 | tf_op jit(solution)/shard_map/all_gather | solution.py:68
  30.9 19.6 %all_gather.33 = bf16[1,64,3072]{2,1,0:T(8,128)(2,1)} all-gather(bf16[1,16,3072]{2,1,0:T(8,128)(2,1)S(1)} %copy-done.23), channel_id=1, replica_groups=mesh['dp'=8,'context'=4] {'context'}, dimensions={1}, use_global_device_ids=true | all-gather | bytes 491520 | tf_op jit(solution)/shard_map/all_gather | solution.py:70
  52.8 24.9 %all-gather.10.cloned.1.call-done = bf16[1,448,3072]{2,1,0:T(8,128)(2,1)} async-done(((bf16[1,112,3072]{2,1,0:T(8,128)(2,1)}), bf16[1,448,3072]{2,1,0:T(8,128)(2,1)}) %all-gather.10.cloned.1.call-update) | async-done | bytes 2752528 | tf_op jit(solution)/shard_map/all_gather | solution.py:67
  81.7 29.0 %all-gather.14.cloned.1.call-done = bf16[3072,4,128]{2,1,0:T(4,128)(2,1)} async-done(((bf16[384,4,128]{2,1,0:T(4,128)(2,1)}), bf16[3072,4,128]{2,1,0:T(4,128)(2,1)}) %all-gather.14.cloned.1.call-update) | async-done | bytes 3145744 | tf_op jit(solution)/shard_map/all_gather | solution.py:76
  110.7 4.1 copy.103
  118.2 26.6 %all-gather.16.cloned.1.call-done = bf16[3072,4,128]{2,1,0:T(4,128)(2,1)} async-done(((bf16[384,4,128]{2,1,0:T(4,128)(2,1)}), bf16[3072,4,128]{2,1,0:T(4,128)(2,1)}) %all-gather.16.cloned.1.call-update) | async-done | bytes 3145744 | tf_op jit(solution)/shard_map/all_gather | solution.py:75
  144.8 4.1 copy.102
  149.0 4.6 copy.89
  156.3 46.9 %all-gather.18.cloned.1.call-done = bf16[1,448,3072]{2,1,0:T(8,128)(2,1)} async-done(((bf16[1,112,3072]{2,1,0:T(8,128)(2,1)}), bf16[1,448,3072]{2,1,0:T(8,128)(2,1)}) %all-gather.18.cloned.1.call-update) | async-done | bytes 2752528 | tf_op jit(solution)/shard_map/all_gather | solution.py:69
  203.2 5.1 fusion.49
  208.3 54.1 %all-gather.8.cloned.1.call-done = bf16[3072,3,4,128]{3,2,1,0:T(4,128)(2,1)} async-done(((bf16[384,3,4,128]{3,2,1,0:T(4,128)(2,1)}), bf16[3072,3,4,128]{3,2,1,0:T(4,128)(2,1)}) %all-gather.8.cloned.1.call-update) | async-done | bytes 9437200 | tf_op jit(solution)/shard_map/all_gather | solution.py:74
  262.4 16.2 %reshape.247 = bf16[3072,1536]{1,0:T(8,128)(2,1)} reshape(bf16[3072,3,4,128]{3,2,1,0:T(4,128)(2,1)} %all-gather.8.cloned.1.call-done) | data formatting | bytes 18874368 | tf_op jit(solution)/shard_map/reshape | solution.py:79
  278.6 5.4 fusion.78
  284.0 38.9 %all-gather.12.cloned.1.call-done = bf16[3072,3,4,128]{3,2,1,0:T(4,128)(2,1)} async-done(((bf16[384,3,4,128]{3,2,1,0:T(4,128)(2,1)}), bf16[3072,3,4,128]{3,2,1,0:T(4,128)(2,1)}) %all-gather.12.cloned.1.call-update) | async-done | bytes 9437200 | tf_op jit(solution)/shard_map/all_gather | solution.py:73
  322.9 15.9 %reshape.248 = bf16[3072,1536]{1,0:T(8,128)(2,1)} reshape(bf16[3072,3,4,128]{3,2,1,0:T(4,128)(2,1)} %all-gather.12.cloned.1.call-done) | data formatting | bytes 18874368 | tf_op jit(solution)/shard_map/reshape | solution.py:78
  338.8 7.6 %fusion.21 = f32[448,1536]{1,0:T(8,128)S(1)} fusion(bf16[3072,1536]{1,0:T(8,128)(2,1)} %reshape.248, bf16[1,448,3072]{2,1,0:T(8,128)(2,1)S(1)} %copy-done.1, f32[3072]{0:T(1024)} %bitcast.215, f32[448]{0:T(512)} %add_rsqrt_fusion.2, f32[448]{0:T(512)S(1)} %broadcast_multiply_fusion.2, f32[3072]{0:T(1024)} %bitcast.213), kind=kOutput, calls=%fused_computation.37 | convolution fusion | flops 4236115968 | bytes 14970368 | tf_op jit(solution)/shard_map/dot_general | solution.py:87
  351.0 3.7 fusion.80
  359.4 8.2 %fusion.46 = f32[512,4,128]{0,2,1:T(8,128)} fusion(f32[4,512,512]{1,2,0:T(8,128)} %fusion.80, f32[512,3,4,128]{0,3,2,1:T(8,128)S(1)} %bitcast.182, f32[512,4]{0,1:T(4,128)} %copy-done.30, f32[4,512,512]{1,2,0:T(8,128)} %copy-done.10, f32[4,512]{1,0:T(4,128)} %copy-done.35), kind=kOutput, calls=%fused_computation.58 | convolution fusion | flops 278399488 | bytes 18898944 | tf_op jit(solution)/shard_map/hij,ihe->jhe/dot_general | solution.py:150
  367.6 10.0 %multiply_reduce_fusion.2 = (f32[512,4]{0,1:T(4,128)}, f32[512,4]{0,1:T(4,128)}, f32[512,4,128]{0,2,1:T(8,128)}) fusion(f32[512,3,4,128]{0,3,2,1:T(8,128)S(1)} %bitcast.183, f32[512,4]{0,1:T(4,128)} %copy-done.30, f32[512,4,128]{0,2,1:T(8,128)} %fusion.46, f32[512,4]{0,1:T(4,128)} %copy-done.29, f32[4,512,512]{1,2,0:T(8,128)} %fusion.80, ...), kind=kOutput, calls=%fused_computation.74 | convolution fusion | flops 279968256 | bytes 22077440 | tf_op jit(solution)/shard_map/hij,jhe->ihe/dot_general | solution.py:149
  384.6 5.7 reshape.258
  390.3 5.8 reshape.259
  418.7 6.2 %convolution_convert_fusion = bf16[3072,1536]{0,1:T(8,128)(2,1)S(1)} fusion(bf16[448,1536]{0,1:T(8,128)(2,1)S(1)} %bitcast.202, bf16[1,448,3072]{2,1,0:T(8,128)(2,1)S(1)} %copy-done.2, f32[3072]{0:T(1024)S(1)} %bitcast.216, f32[448]{0:T(512)S(1)} %copy-done.38, f32[3072]{0:T(1024)S(1)} %bitcast.214, f32[448]{0:T(512)S(1)} %broadcast_multiply_fusion.2), kind=kOutput, calls=%fused_computation.3 | convolution fusion | flops 4240834560 | bytes 13594112 | tf_op jit(solution)/shard_map/dot_general | solution.py:31
  424.9 7.6 %pad_maximum_fusion = bf16[3072,2560]{0,1:T(8,128)(2,1)} fusion(bf16[3072,512]{0,1:T(8,128)(2,1)S(1)} %convolution_convert_fusion.2, bf16[3072,512]{0,1:T(8,128)(2,1)S(1)} %convolution_convert_fusion.3, bf16[3072,1536]{0,1:T(8,128)(2,1)S(1)} %convolution_convert_fusion), kind=kLoop, calls=%fused_computation.2 | loop fusion | flops 47185920 | bytes 31457280 | tf_op jit(solution)/shard_map/concatenate | solution.py:185
  432.5 20.1 %copy.92 = bf16[3072,2560]{1,0:T(8,128)(2,1)} copy(bf16[3072,2560]{0,1:T(8,128)(2,1)} %pad_maximum_fusion) | data formatting | bytes 31457280
  457.0 18.9 %reduce.2 = bf16[3072,64]{1,0:T(8,128)(2,1)} reduce(bf16[3072,1,64]{2,1,0:T(2,128)(2,1)} %bitcast.193, bf16[]{:T(256)} %broadcast.209), dimensions={1}, to_apply=%bitcast.152.reduce_sub_computation | reduce | bytes 786434
  478.6 12.6 %all_to_all.18 = bf16[8,2,12288]{2,1,0:T(2,128)(2,1)} all-to-all(bf16[8,2,12288]{2,1,0:T(2,128)(2,1)} %reshape.268), channel_id=1, replica_groups=mesh['dp'=8,'context'=4] {'dp'}, dimensions={0} | all-to-all | bytes 786432 | tf_op jit(solution)/shard_map/all_to_all | solution.py:189
  491.2 3.7 reshape.269
  500.1 7.3 %fusion.103 = (bf16[3072]{0:T(1024)(128)(2,1)S(1)}, bf16[3072]{0:T(1024)(128)(2,1)S(1)}) fusion(f32[64]{0:T(128)} %copy-done.37, f32[64]{0:T(128)} %copy-done.36, bf16[1,64,3072]{2,1,0:T(8,128)(2,1)S(1)} %all_gather.27, bf16[64,1536]{0,1:T(8,128)(2,1)S(1)} %bitcast.196, bf16[3072,1536]{1,0:T(8,128)(2,1)} %reshape.247), kind=kOutput, calls=%fused_computation.131 | convolution fusion | flops 605153280 | bytes 10039808 | tf_op jit(solution)/shard_map/dot_general | solution.py:37
  507.5 9.5 %fusion.102 = (bf16[3072]{0:T(1024)(128)(2,1)S(1)}, bf16[3072]{0:T(1024)(128)(2,1)S(1)}) fusion(f32[448]{0:T(512)S(1)} %copy-done.39, f32[448]{0:T(512)S(1)} %broadcast_multiply_fusion.2, bf16[1,448,3072]{2,1,0:T(8,128)(2,1)S(1)} %copy-done.2, bf16[448,1536]{0,1:T(8,128)(2,1)S(1)} %bitcast.203, bf16[3072,1536]{1,0:T(8,128)(2,1)} %reshape.248), kind=kOutput, calls=%fused_computation.130 | convolution fusion | flops 4236109824 | bytes 13581824 | tf_op jit(solution)/shard_map/dot_general | solution.py:37
  517.0 4.0 convolution_convert_fusion.1
  527.6 19.2 %all-reduce = (bf16[1,3,3072]{2,0,1:T(2,128)(2,1)S(1)}, bf16[1,3,3072]{2,0,1:T(2,128)(2,1)S(1)}) all-reduce(bf16[1,3,3072]{2,0,1:T(2,128)(2,1)S(1)} %broadcast_in_dim.37, bf16[1,3,3072]{2,0,1:T(2,128)(2,1)S(1)} %broadcast_in_dim.39), channel_id=1, replica_groups=mesh['dp'=8,'context'=4] {'context'}, use_global_device_ids=true, to_apply=%region_16.0 | all-reduce | flops 18432 | bytes 73728 | tf_op jit(solution)/shard_map/psum | solution.py:178
  548.1 39.9 %reduce-scatter.7.cloned.1.call-done = bf16[384,2560]{1,0:T(8,128)(2,1)} async-done(((bf16[3072,2560]{1,0:T(8,128)(2,1)}), bf16[384,2560]{1,0:T(8,128)(2,1)}) %reduce-scatter.7.cloned.1.call-update) | async-done | bytes 1966096
  (171 shorter events, 86.7 us)
Async XLA Ops:
  7.2 4.0 copy-start.26
  7.2 4.1 copy-start.27
  7.2 4.1 copy-start.28
  7.2 23.7 %copy-start.23 = (bf16[1,16,3072]{2,1,0:T(8,128)(2,1)S(1)}, bf16[1,16,3072]{2,1,0:T(8,128)(2,1)}, u32[]{:S(2)}) copy-start(bf16[1,16,3072]{2,1,0:T(8,128)(2,1)} %param.19) | copy-start | bytes 294916
  7.2 70.4 %all-gather.10.cloned.1.call-start = ((), (), s32[]{:S(2)}) async-start(), calls=%async_computation.4 | async-start | bytes 3440640 | tf_op jit(solution)/shard_map/all_gather | solution.py:67
  7.9 102.8 %all-gather.14.cloned.1.call-start = ((), (), s32[]{:S(2)}) async-start(), calls=%async_computation.6 | async-start | bytes 3538944 | tf_op jit(solution)/shard_map/all_gather | solution.py:76
  8.7 136.1 %all-gather.16.cloned.1.call-start = ((), (), s32[]{:S(2)}) async-start(), calls=%async_computation.7 | async-start | bytes 3538944 | tf_op jit(solution)/shard_map/all_gather | solution.py:75
  9.4 193.8 %all-gather.18.cloned.1.call-start = ((), (), s32[]{:S(2)}) async-start(), calls=%async_computation.9 | async-start | bytes 3440640 | tf_op jit(solution)/shard_map/all_gather | solution.py:69
  10.0 252.4 %all-gather.8.cloned.1.call-start = ((), (), s32[]{:S(2)}) async-start(), calls=%async_computation.3 | async-start | bytes 10616832 | tf_op jit(solution)/shard_map/all_gather | solution.py:74
  10.6 312.3 %all-gather.12.cloned.1.call-start = ((), (), s32[]{:S(2)}) async-start(), calls=%async_computation.5 | async-start | bytes 10616832 | tf_op jit(solution)/shard_map/all_gather | solution.py:73
  11.2 505.8 %all-gather.20.cloned.1.call-start = ((), (), s32[]{:S(2)}) async-start(), calls=%async_computation.10 | async-start | bytes 1769472 | tf_op jit(solution)/shard_map/all_gather | solution.py:190
  30.6 84.2 %copy-start.36 = (f32[64]{0:T(128)}, f32[64]{0:T(128)S(1)}, u32[]{:S(2)}) copy-start(f32[64]{0:T(128)S(1)} %broadcast_multiply_fusion.3) | copy-start | bytes 772
  50.5 64.4 %copy-start.37 = (f32[64]{0:T(128)}, f32[64]{0:T(128)S(1)}, u32[]{:S(2)}) copy-start(f32[64]{0:T(128)S(1)} %add_rsqrt_fusion.3) | copy-start | bytes 772
  208.3 70.3 %copy-start.4 = (bf16[1,64,3072]{2,1,0:T(8,128)(2,1)S(1)}, bf16[1,64,3072]{2,1,0:T(8,128)(2,1)}, u32[]{:S(2)}) copy-start(bf16[1,64,3072]{2,1,0:T(8,128)(2,1)} %fusion.63) | copy-start | bytes 1179652
  284.0 54.8 %copy-start.1 = (bf16[1,448,3072]{2,1,0:T(8,128)(2,1)S(1)}, bf16[1,448,3072]{2,1,0:T(8,128)(2,1)}, u32[]{:S(2)}) copy-start(bf16[1,448,3072]{2,1,0:T(8,128)(2,1)} %all-gather.10.cloned.1.call-done) | copy-start | bytes 8257540
  351.0 4.7 copy-start.29
  351.0 4.7 copy-start.30
  354.7 2.9 copy-start.22
  354.7 2.9 copy-start.25
  377.6 4.3 copy-start.16
  384.5 139.8 %reduce-scatter.5.cloned.1.call-start = ((), (), s32[]{:S(2)}) async-start(), calls=%async_computation.8 | async-start | bytes 3932160 | tf_op jit(solution)/shard_map/reduce_scatter | solution.py:116
  399.1 10.1 %copy-start.13 = (bf16[3072,512,1]{1,0,2:T(8,128)(2,1)S(1)}, bf16[3072,512,1]{1,0,2:T(8,128)(2,1)}, u32[]{:S(2)}) copy-start(bf16[3072,512,1]{1,0,2:T(8,128)(2,1)} %reshape.259) | copy-start | bytes 9437188
  414.1 173.9 %reduce-scatter.7.cloned.1.call-start = ((), (), s32[]{:S(2)}) async-start(), calls=%async_computation.11 | async-start | bytes 17694720
  415.1 3.6 copy-start.19
  475.9 24.2 %copy-start.11 = (bf16[64,3,4,128]{0,3,2,1:T(8,128)(2,1)S(1)}, bf16[64,3,4,128]{0,3,2,1:T(8,128)(2,1)}, u32[]{:S(2)}) copy-start(bf16[64,3,4,128]{0,3,2,1:T(8,128)(2,1)} %pad_maximum_fusion.5) | copy-start | bytes 589828
  500.1 7.3 %copy-start.20 = (bf16[448,3,4,128]{0,3,2,1:T(8,128)(2,1)S(1)}, bf16[448,3,4,128]{0,3,2,1:T(8,128)(2,1)}, u32[]{:S(2)}) copy-start(bf16[448,3,4,128]{0,3,2,1:T(8,128)(2,1)} %copy-done.19) | copy-start | bytes 4128772
  500.1 7.4 %copy-start.39 = (f32[448]{0:T(512)S(1)}, f32[448]{0:T(512)}, u32[]{:S(2)}) copy-start(f32[448]{0:T(512)} %add_rsqrt_fusion.2) | copy-start | bytes 5380
  507.4 9.6 %copy-start.18 = (bf16[1,64,8,384]{3,1,2,0:T(8,128)(2,1)S(1)}, bf16[1,64,8,384]{3,1,2,0:T(8,128)(2,1)}, u32[]{:S(2)}) copy-start(bf16[1,64,8,384]{3,1,2,0:T(8,128)(2,1)} %copy.74) | copy-start | bytes 1179652
  522.4 3.2 copy-start.24
  522.4 3.9 copy-start.14
  522.4 3.9 copy-start.32
  593.4 3.6 copy-start.3
  (18 other events, 31.4 us)
Sparse Core Ops, SparseCore 0:
  9.6 68.0 all-gather.9
  79.5 31.1 all-gather.13
  112.6 32.1 all-gather.15
  146.3 56.9 all-gather.17
  204.9 57.4 all-gather.7
  264.1 58.6 all-gather.11
  384.6 25.6 all-gather.19
  414.2 60.3 reduce-scatter.4
  478.1 109.8 reduce-scatter.6
where the time goes:
time: 612 us; the launch traced here: 606 us
  waiting for transfers between devices  264 us (43%)
  local copies, waits for them, and re-layouts  126 us (21%)
  matrix products  84.2 us (14%)
  blocking collectives  70.6 us (12%)
  other arithmetic  46.6 us (8%)
  between operations  14.7 us (2%)
    all_gather x1, waiting for transfers between devices, body(): lax.all_gather(text_qkv_weight, 'dp', axis=0, tiled=True)  54.1 us
    unnamed x93, local copies, waits for them, and re-layouts  51.8 us
    all_gather x1, waiting for transfers between devices, body(): lax.all_gather(image_slope, 'context', axis=1, tiled=True)  46.9 us
    unnamed x10, waiting for transfers between devices  43.6 us
    all_gather x1, waiting for transfers between devices, body(): lax.all_gather(image_qkv_weight, 'dp', axis=0, tiled=True)  38.9 us
    all_gather x1, waiting for transfers between devices, body(): lax.all_gather(text_out_weight, 'dp', axis=0, tiled=True)  29 us
    all_gather x1, waiting for transfers between devices, body(): lax.all_gather(image_out_weight, 'dp', axis=0, tiled=True)  26.6 us
    all_gather x1, waiting for transfers between devices, body(): lax.all_gather(image_tokens, 'context', axis=1, tiled=True)  24.9 us
  transfers between devices with their start and end apart: 9, of which 7 were waited for; matrix products, arithmetic and copies ran while one was open for 30% of the time, Pallas kernels for 0%

commit v1 on v0

--- a/solution.py
+++ b/solution.py
@@ -2,6 +2,7 @@
 import jax.numpy as jnp
 from jax import lax
 from jax.sharding import PartitionSpec as P
+from jax.lax import axis_index, axis_size, ppermute
 
 norm_eps = 1e-06
 
@@ -63,10 +64,35 @@
     triple = 3 * inner_width
     text_rows = own_text * groups
     score_scale = head_size ** (-0.5)
+
+    def return_all_the_cube(sample):
+        inter = axis_size("context")
+        e_next = axis_index("context")
+        r1, passed, s_next = (inter, e_next, sample.shape[1])
+        rack = [k * r1 if h == 1 else k for h, k in enumerate(sample.shape)]
+        e_now = lax.dynamic_update_slice_in_dim(
+            jnp.zeros(rack, sample.dtype), sample, passed * s_next, axis=1
+        )
+        q_next = row_out = sample
+        for at in range(1, r1 // 2 + 1):
+            f_now = map(lambda h: (h, (h + 1) % r1), range(r1))
+            r_now = list(f_now)
+            q_next = ppermute(q_next, "context", r_now)
+            e_now = lax.dynamic_update_slice_in_dim(
+                e_now, q_next, (passed - at) % r1 * s_next, axis=1
+            )
+            if 2 * at < r1:
+                kept_arr = map(lambda h: (h, (h - 1) % r1), range(r1))
+                row_out = ppermute(row_out, "context", perm=list(kept_arr))
+                e_now = lax.dynamic_update_slice_in_dim(
+                    e_now, row_out, (passed + at) % r1 * s_next, axis=1
+                )
+        return e_now
+
     whole_image, whole_text, slopes_image, slopes_text = (
         lax.all_gather(image_tokens, "context", axis=1, tiled=True),
         lax.all_gather(text_tokens, "context", axis=1, tiled=True),
-        lax.all_gather(image_slope, "context", axis=1, tiled=True),
+        return_all_the_cube(image_slope),
         lax.all_gather(text_slope, "context", axis=1, tiled=True),
     )
     full_q_image, full_q_text, full_o_image, full_o_text = (

time: 612 us -> 580 us (0.948)
  waiting for transfers between devices: 264 us -> 165 us
  blocking collectives: 70.6 us -> 124 us
  starting transfers between devices: 0.35 us -> 6.49 us
    all_gather x1, blocking collectives: 19.2 us -> 73.2 us  [body(): lax.all_gather(text_tokens, 'context', axis=1, tiled=True)]
    all_gather x1 -> x0, waiting for transfers between devices: 46.9 us -> none  [body(): lax.all_gather(image_slope, 'context', axis=1, tiled=True)]
    all_gather x1, waiting for transfers between devices: 29 us -> 3.57 us  [body(): lax.all_gather(text_out_weight, 'dp', axis=0, tiled=True)]
    all_gather x1, waiting for transfers between devices: 24.9 us -> 0.01 us  [body(): lax.all_gather(image_tokens, 'context', axis=1, tiled=True)]
    all_gather x1, waiting for transfers between devices: 54.1 us -> 43.8 us  [body(): lax.all_gather(text_qkv_weight, 'dp', axis=0, tiled=True)]
    ppermute x0 -> x3, waiting for transfers between devices: none -> 9.9 us  [the longest x2 9.9 us: return_all_the_cube(): q_next = ppermute(q_next, 'context', r_now)]
    ppermute x0 -> x3, starting transfers between devices: none -> 6.18 us  [the longest x1 5.13 us: return_all_the_cube(): row_out = ppermute(row_out, 'context', perm=list(kept_arr))]
    unnamed x93 -> x91, local copies, waits for them, and re-layouts: 51.8 us -> 49.9 us
  transfers between devices with their start and end apart: 9 -> 11, of which waited for: 7 -> 6; matrix products, arithmetic and copies ran while one was open for 30% -> 33% of each run, Pallas kernels for 0% -> 0%
where the time goes in v1:
time: 580 us; the launch traced here: 574 us
  waiting for transfers between devices  165 us (28%)
  local copies, waits for them, and re-layouts  129 us (22%)
  blocking collectives  124 us (21%)
  matrix products  86.2 us (15%)
  other arithmetic  48.2 us (8%)
  between operations  15 us (3%)
  starting transfers between devices  6.49 us (1%)
    all_gather x1, blocking collectives, body(): lax.all_gather(text_tokens, 'context', axis=1, tiled=True)  73.2 us
    unnamed x91, local copies, waits for them, and re-layouts  49.9 us
    all_gather x1, waiting for transfers between devices, body(): lax.all_gather(text_qkv_weight, 'dp', axis=0, tiled=True)  43.8 us
    unnamed x9, waiting for transfers between devices  42 us
    all_gather x1, waiting for transfers between devices, body(): lax.all_gather(image_qkv_weight, 'dp', axis=0, tiled=True)  38.9 us
    all_gather x1, waiting for transfers between devices, body(): lax.all_gather(image_out_weight, 'dp', axis=0, tiled=True)  26.6 us
    dot_general x4, matrix products, contract_last(): lax.dot_general(left_side, right_side, (((1,), (1,)), ((), ())), preferre...  22.8 us
    psum x1, blocking collectives, body(): lax.psum(part_image.astype(jnp.bfloat16), 'context').astype(jnp.float32)  20.3 us
  transfers between devices with their start and end apart: 11, of which 6 were waited for; matrix products, arithmetic and copies ran while one was open for 33% of the time, Pallas kernels for 0%

profile of v1, /device:TPU:0, one launch (start us, length us, event | category | flops | bytes accessed | tf_op | source)
XLA Modules:
  0.0 573.6 jit_solution(9897960337860694268)
XLA Ops:
  10.6 5.1 collective-permute-start.1
  17.3 73.2 %all_gather.24 = bf16[1,64,3072]{2,1,0:T(8,128)(2,1)S(1)} all-gather(bf16[1,16,3072]{2,1,0:T(8,128)(2,1)} %param.11), channel_id=1, replica_groups=mesh['dp'=8,'context'=4] {'context'}, dimensions={1}, use_global_device_ids=true | all-gather | bytes 491520 | tf_op jit(solution)/shard_map/all_gather | solution.py:94
  90.9 17.7 %all_gather.30 = bf16[1,64,3072]{2,1,0:T(8,128)(2,1)} all-gather(bf16[1,16,3072]{2,1,0:T(8,128)(2,1)S(1)} %copy-done.24), channel_id=1, replica_groups=mesh['dp'=8,'context'=4] {'context'}, dimensions={1}, use_global_device_ids=true | all-gather | bytes 491520 | tf_op jit(solution)/shard_map/all_gather | solution.py:96
  116.6 9.9 %collective-permute-done.2 = bf16[1,112,3072]{2,1,0:T(8,128)(2,1)S(1)} collective-permute-done((bf16[1,112,3072]{2,1,0:T(8,128)(2,1)S(1)}, bf16[1,112,3072]{2,1,0:T(8,128)(2,1)S(1)}, u32[]{:S(2)}, u32[]{:S(2)}) %collective-permute-start.2) | collective-permute-done | bytes 688160 | tf_op jit(solution)/shard_map/ppermute | solution.py:80
  135.1 4.1 copy.103
  142.6 26.6 %all-gather.15.cloned.1.call-done = bf16[3072,4,128]{2,1,0:T(4,128)(2,1)} async-done(((bf16[384,4,128]{2,1,0:T(4,128)(2,1)}), bf16[3072,4,128]{2,1,0:T(4,128)(2,1)}) %all-gather.15.cloned.1.call-update) | async-done | bytes 3145744 | tf_op jit(solution)/shard_map/all_gather | solution.py:101
  169.2 4.1 copy.102
  173.3 4.6 copy.89
  180.8 5.1 fusion.47
  185.9 43.8 %all-gather.7.cloned.1.call-done = bf16[3072,3,4,128]{3,2,1,0:T(4,128)(2,1)} async-done(((bf16[384,3,4,128]{3,2,1,0:T(4,128)(2,1)}), bf16[3072,3,4,128]{3,2,1,0:T(4,128)(2,1)}) %all-gather.7.cloned.1.call-update) | async-done | bytes 9437200 | tf_op jit(solution)/shard_map/all_gather | solution.py:100
  229.7 16.2 %reshape.239 = bf16[3072,1536]{1,0:T(8,128)(2,1)} reshape(bf16[3072,3,4,128]{3,2,1,0:T(4,128)(2,1)} %all-gather.7.cloned.1.call-done) | data formatting | bytes 18874368 | tf_op jit(solution)/shard_map/reshape | solution.py:105
  245.9 5.4 fusion.76
  251.2 38.9 %all-gather.11.cloned.1.call-done = bf16[3072,3,4,128]{3,2,1,0:T(4,128)(2,1)} async-done(((bf16[384,3,4,128]{3,2,1,0:T(4,128)(2,1)}), bf16[3072,3,4,128]{3,2,1,0:T(4,128)(2,1)}) %all-gather.11.cloned.1.call-update) | async-done | bytes 9437200 | tf_op jit(solution)/shard_map/all_gather | solution.py:99
  290.1 15.9 %reshape.240 = bf16[3072,1536]{1,0:T(8,128)(2,1)} reshape(bf16[3072,3,4,128]{3,2,1,0:T(4,128)(2,1)} %all-gather.11.cloned.1.call-done) | data formatting | bytes 18874368 | tf_op jit(solution)/shard_map/reshape | solution.py:104
  306.0 7.6 %fusion.21 = f32[448,1536]{1,0:T(8,128)S(1)} fusion(bf16[3072,1536]{1,0:T(8,128)(2,1)} %reshape.240, bf16[1,448,3072]{2,1,0:T(8,128)(2,1)S(1)} %copy-done.1, f32[3072]{0:T(1024)} %bitcast.218, f32[448]{0:T(512)} %add_rsqrt_fusion.2, f32[448]{0:T(512)S(1)} %broadcast_multiply_fusion.2, f32[3072]{0:T(1024)} %bitcast.216), kind=kOutput, calls=%fused_computation.37 | convolution fusion | flops 4236115968 | bytes 14970368 | tf_op jit(solution)/shard_map/dot_general | solution.py:113
  318.2 3.7 fusion.78
  326.6 8.2 %fusion.44 = f32[512,4,128]{0,2,1:T(8,128)} fusion(f32[4,512,512]{1,2,0:T(8,128)} %fusion.78, f32[512,3,4,128]{0,3,2,1:T(8,128)S(1)} %bitcast.185, f32[512,4]{0,1:T(4,128)} %copy-done.30, f32[4,512,512]{1,2,0:T(8,128)} %copy-done.10, f32[4,512]{1,0:T(4,128)} %copy-done.35), kind=kOutput, calls=%fused_computation.56 | convolution fusion | flops 278399488 | bytes 18898944 | tf_op jit(solution)/shard_map/hij,ihe->jhe/dot_general | solution.py:176
  334.9 10.0 %multiply_reduce_fusion.3 = (f32[512,4]{0,1:T(4,128)}, f32[512,4]{0,1:T(4,128)}, f32[512,4,128]{0,2,1:T(8,128)}) fusion(f32[512,3,4,128]{0,3,2,1:T(8,128)S(1)} %bitcast.186, f32[512,4]{0,1:T(4,128)} %copy-done.30, f32[512,4,128]{0,2,1:T(8,128)} %fusion.44, f32[512,4]{0,1:T(4,128)} %copy-done.29, f32[4,512,512]{1,2,0:T(8,128)} %fusion.78, ...), kind=kOutput, calls=%fused_computation.72 | convolution fusion | flops 279968256 | bytes 22077440 | tf_op jit(solution)/shard_map/hij,jhe->ihe/dot_general | solution.py:175
  351.8 5.7 reshape.249
  357.5 5.8 %reshape.250 = bf16[3072,512,1]{1,0,2:T(8,128)(2,1)} reshape(bf16[3072,4,128]{2,1,0:T(4,128)(2,1)} %all-gather.15.cloned.1.call-done) | data formatting | bytes 6291456 | tf_op jit(solution)/shard_map/reshape | solution.py:106
  383.4 3.8 convolution_convert_fusion.3
  387.2 6.1 %convolution_convert_fusion = bf16[3072,1536]{0,1:T(8,128)(2,1)S(1)} fusion(bf16[448,1536]{0,1:T(8,128)(2,1)S(1)} %bitcast.205, bf16[1,448,3072]{2,1,0:T(8,128)(2,1)S(1)} %copy-done.2, f32[3072]{0:T(1024)S(1)} %bitcast.219, f32[448]{0:T(512)S(1)} %copy-done.38, f32[3072]{0:T(1024)S(1)} %bitcast.217, f32[448]{0:T(512)S(1)} %broadcast_multiply_fusion.2), kind=kOutput, calls=%fused_computation.3 | convolution fusion | flops 4240834560 | bytes 13594112 | tf_op jit(solution)/shard_map/dot_general | solution.py:32
  393.3 7.7 %pad_maximum_fusion = bf16[3072,2560]{0,1:T(8,128)(2,1)} fusion(bf16[3072,512]{0,1:T(8,128)(2,1)S(1)} %convolution_convert_fusion.2, bf16[3072,512]{0,1:T(8,128)(2,1)S(1)} %convolution_convert_fusion.3, bf16[3072,1536]{0,1:T(8,128)(2,1)S(1)} %convolution_convert_fusion), kind=kLoop, calls=%fused_computation.2 | loop fusion | flops 47185920 | bytes 31457280 | tf_op jit(solution)/shard_map/concatenate | solution.py:211
  401.0 19.2 %copy.92 = bf16[3072,2560]{1,0:T(8,128)(2,1)} copy(bf16[3072,2560]{0,1:T(8,128)(2,1)} %pad_maximum_fusion) | data formatting | bytes 31457280
  424.6 18.9 %reduce.2 = bf16[3072,64]{1,0:T(8,128)(2,1)} reduce(bf16[3072,1,64]{2,1,0:T(2,128)(2,1)} %bitcast.196, bf16[]{:T(256)} %broadcast.206), dimensions={1}, to_apply=%bitcast.155.reduce_sub_computation | reduce | bytes 786434
  446.2 12.6 %all_to_all.18 = bf16[8,2,12288]{2,1,0:T(2,128)(2,1)} all-to-all(bf16[8,2,12288]{2,1,0:T(2,128)(2,1)} %reshape.259), channel_id=1, replica_groups=mesh['dp'=8,'context'=4] {'dp'}, dimensions={0} | all-to-all | bytes 786432 | tf_op jit(solution)/shard_map/all_to_all | solution.py:215
  458.8 3.7 reshape.260
  467.2 7.3 %fusion.101 = (bf16[3072]{0:T(1024)(128)(2,1)S(1)}, bf16[3072]{0:T(1024)(128)(2,1)S(1)}) fusion(f32[64]{0:T(128)} %copy-done.37, f32[64]{0:T(128)} %copy-done.36, bf16[1,64,3072]{2,1,0:T(8,128)(2,1)S(1)} %all_gather.24, bf16[64,1536]{0,1:T(8,128)(2,1)S(1)} %bitcast.199, bf16[3072,1536]{1,0:T(8,128)(2,1)} %reshape.239), kind=kOutput, calls=%fused_computation.133 | convolution fusion | flops 605153280 | bytes 10039808 | tf_op jit(solution)/shard_map/dot_general | solution.py:38
  474.6 9.5 %fusion.100 = (bf16[3072]{0:T(1024)(128)(2,1)S(1)}, bf16[3072]{0:T(1024)(128)(2,1)S(1)}) fusion(f32[448]{0:T(512)S(1)} %copy-done.39, f32[448]{0:T(512)S(1)} %broadcast_multiply_fusion.2, bf16[1,448,3072]{2,1,0:T(8,128)(2,1)S(1)} %copy-done.2, bf16[448,1536]{0,1:T(8,128)(2,1)S(1)} %bitcast.206, bf16[3072,1536]{1,0:T(8,128)(2,1)} %reshape.240), kind=kOutput, calls=%fused_computation.132 | convolution fusion | flops 4236109824 | bytes 13581824 | tf_op jit(solution)/shard_map/dot_general | solution.py:38
  484.1 4.0 convolution_convert_fusion.1
  494.7 20.3 %all-reduce = (bf16[1,3,3072]{2,0,1:T(2,128)(2,1)S(1)}, bf16[1,3,3072]{2,0,1:T(2,128)(2,1)S(1)}) all-reduce(bf16[1,3,3072]{2,0,1:T(2,128)(2,1)S(1)} %broadcast_in_dim.38, bf16[1,3,3072]{2,0,1:T(2,128)(2,1)S(1)} %broadcast_in_dim.40), channel_id=1, replica_groups=mesh['dp'=8,'context'=4] {'context'}, use_global_device_ids=true, to_apply=%region_16.17 | all-reduce | flops 18432 | bytes 73728 | tf_op jit(solution)/shard_map/psum | solution.py:204
  516.3 38.8 %reduce-scatter.7.cloned.1.call-done = bf16[384,2560]{1,0:T(8,128)(2,1)} async-done(((bf16[3072,2560]{1,0:T(8,128)(2,1)}), bf16[384,2560]{1,0:T(8,128)(2,1)}) %reduce-scatter.7.cloned.1.call-update) | async-done | bytes 1966096
  (177 shorter events, 95.0 us)
Async XLA Ops:
  7.2 101.4 %copy-start.27 = (bf16[1,3,3072]{2,1,0:T(4,128)(2,1)S(1)}, bf16[1,3,3072]{2,1,0:T(4,128)(2,1)}, u32[]{:S(2)}) copy-start(bf16[1,3,3072]{2,1,0:T(4,128)(2,1)} %param.12) | copy-start | bytes 55300
  7.2 102.0 %copy-start.28 = (bf16[1,3,3072]{2,1,0:T(4,128)(2,1)S(1)}, bf16[1,3,3072]{2,1,0:T(4,128)(2,1)}, u32[]{:S(2)}) copy-start(bf16[1,3,3072]{2,1,0:T(4,128)(2,1)} %param.13) | copy-start | bytes 55300
  7.2 83.7 %copy-start.24 = (bf16[1,16,3072]{2,1,0:T(8,128)(2,1)S(1)}, bf16[1,16,3072]{2,1,0:T(8,128)(2,1)}, u32[]{:S(2)}) copy-start(bf16[1,16,3072]{2,1,0:T(8,128)(2,1)} %param.19) | copy-start | bytes 294916
  7.2 120.2 %all-gather.9.cloned.1.call-start = ((), (), s32[]{:S(2)}) async-start(), calls=%async_computation.4 | async-start | bytes 3440640 | tf_op jit(solution)/shard_map/all_gather | solution.py:93
  7.9 103.9 %copy-start.14 = (bf16[1,112,3072]{2,1,0:T(8,128)(2,1)S(1)}, bf16[1,112,3072]{2,1,0:T(8,128)(2,1)}, u32[]{:S(2)}) copy-start(bf16[1,112,3072]{2,1,0:T(8,128)(2,1)} %param.18) | copy-start | bytes 2064388
  7.9 127.1 %all-gather.13.cloned.1.call-start = ((), (), s32[]{:S(2)}) async-start(), calls=%async_computation.6 | async-start | bytes 3538944 | tf_op jit(solution)/shard_map/all_gather | solution.py:102
  8.7 160.5 %all-gather.15.cloned.1.call-start = ((), (), s32[]{:S(2)}) async-start(), calls=%async_computation.7 | async-start | bytes 3538944 | tf_op jit(solution)/shard_map/all_gather | solution.py:101
  9.4 220.2 %all-gather.7.cloned.1.call-start = ((), (), s32[]{:S(2)}) async-start(), calls=%async_computation.3 | async-start | bytes 10616832 | tf_op jit(solution)/shard_map/all_gather | solution.py:100
  10.0 280.1 %all-gather.11.cloned.1.call-start = ((), (), s32[]{:S(2)}) async-start(), calls=%async_computation.5 | async-start | bytes 10616832 | tf_op jit(solution)/shard_map/all_gather | solution.py:99
  10.6 473.5 %all-gather.17.cloned.1.call-start = ((), (), s32[]{:S(2)}) async-start(), calls=%async_computation.9 | async-start | bytes 1769472 | tf_op jit(solution)/shard_map/all_gather | solution.py:216
  10.6 105.0 %collective-permute-start.1 = (bf16[1,112,3072]{2,1,0:T(8,128)(2,1)}, bf16[1,112,3072]{2,1,0:T(8,128)(2,1)S(1)}, u32[]{:S(2)}, u32[]{:S(2)}) collective-permute-start(bf16[1,112,3072]{2,1,0:T(8,128)(2,1)} %param.18), channel_id=1, source_target_pairs={{0,3},{1,0},{2,1},{3,2},{4,7},{5,4},{6,5},{7,6},{8,11},{9,8},{10,9... | collective-permute-start | bytes 2064392 | tf_op jit(solution)/shard_map/ppermute | solution.py:86
  15.8 97.9 %collective-permute-start = (bf16[1,112,3072]{2,1,0:T(8,128)(2,1)}, bf16[1,112,3072]{2,1,0:T(8,128)(2,1)S(1)}, u32[]{:S(2)}, u32[]{:S(2)}) collective-permute-start(bf16[1,112,3072]{2,1,0:T(8,128)(2,1)} %param.18), channel_id=1, source_target_pairs={{0,1},{1,2},{2,3},{3,0},{4,5},{5,6},{6,7},{7,4},{8,9},{9,10},{10,1... | collective-permute-start | bytes 2064392 | tf_op jit(solution)/shard_map/ppermute | solution.py:80
  90.6 23.1 %copy-start.36 = (f32[64]{0:T(128)}, f32[64]{0:T(128)S(1)}, u32[]{:S(2)}) copy-start(f32[64]{0:T(128)S(1)} %broadcast_multiply_fusion.3) | copy-start | bytes 772
  108.6 5.1 copy-start.37
  113.7 12.8 %collective-permute-start.2 = (bf16[1,112,3072]{2,1,0:T(8,128)(2,1)S(1)}, bf16[1,112,3072]{2,1,0:T(8,128)(2,1)S(1)}, u32[]{:S(2)}, u32[]{:S(2)}) collective-permute-start(bf16[1,112,3072]{2,1,0:T(8,128)(2,1)S(1)} %collective-permute-done), channel_id=1, source_target_pairs={{0,1},{1,2},{2,3},{3,0},{4,5},{5,6},{6,7},{7,4},{8,9},{9,10},{10,1... | collective-permute-start | bytes 2064392 | tf_op jit(solution)/shard_map/ppermute | solution.py:80
  185.9 60.0 %copy-start.4 = (bf16[1,64,3072]{2,1,0:T(8,128)(2,1)S(1)}, bf16[1,64,3072]{2,1,0:T(8,128)(2,1)}, u32[]{:S(2)}) copy-start(bf16[1,64,3072]{2,1,0:T(8,128)(2,1)} %fusion.61) | copy-start | bytes 1179652
  251.2 54.8 %copy-start.1 = (bf16[1,448,3072]{2,1,0:T(8,128)(2,1)S(1)}, bf16[1,448,3072]{2,1,0:T(8,128)(2,1)}, u32[]{:S(2)}) copy-start(bf16[1,448,3072]{2,1,0:T(8,128)(2,1)} %all-gather.9.cloned.1.call-done) | copy-start | bytes 8257540
  318.2 4.7 copy-start.29
  318.2 4.7 copy-start.30
  344.8 4.3 copy-start.17
  351.8 139.6 %reduce-scatter.5.cloned.1.call-start = ((), (), s32[]{:S(2)}) async-start(), calls=%async_computation.8 | async-start | bytes 3932160 | tf_op jit(solution)/shard_map/reduce_scatter | solution.py:142
  366.4 10.1 %copy-start.13 = (bf16[3072,512,1]{1,0,2:T(8,128)(2,1)S(1)}, bf16[3072,512,1]{1,0,2:T(8,128)(2,1)}, u32[]{:S(2)}) copy-start(bf16[3072,512,1]{1,0,2:T(8,128)(2,1)} %reshape.250) | copy-start | bytes 9437188
  381.3 173.9 %reduce-scatter.7.cloned.1.call-start = ((), (), s32[]{:S(2)}) async-start(), calls=%async_computation.10 | async-start | bytes 17694720
  382.3 4.8 copy-start.20
  383.3 3.8 copy-start.2
  383.3 3.8 copy-start.33
  443.5 23.7 %copy-start.11 = (bf16[64,3,4,128]{0,3,2,1:T(8,128)(2,1)S(1)}, bf16[64,3,4,128]{0,3,2,1:T(8,128)(2,1)}, u32[]{:S(2)}) copy-start(bf16[64,3,4,128]{0,3,2,1:T(8,128)(2,1)} %pad_maximum_fusion.5) | copy-start | bytes 589828
  467.2 7.4 %copy-start.21 = (bf16[448,3,4,128]{0,3,2,1:T(8,128)(2,1)S(1)}, bf16[448,3,4,128]{0,3,2,1:T(8,128)(2,1)}, u32[]{:S(2)}) copy-start(bf16[448,3,4,128]{0,3,2,1:T(8,128)(2,1)} %copy-done.20) | copy-start | bytes 4128772
  467.2 7.4 %copy-start.39 = (f32[448]{0:T(512)S(1)}, f32[448]{0:T(512)}, u32[]{:S(2)}) copy-start(f32[448]{0:T(512)} %add_rsqrt_fusion.2) | copy-start | bytes 5380
  474.6 9.6 %copy-start.19 = (bf16[1,64,8,384]{3,1,2,0:T(8,128)(2,1)S(1)}, bf16[1,64,8,384]{3,1,2,0:T(8,128)(2,1)}, u32[]{:S(2)}) copy-start(bf16[1,64,8,384]{3,1,2,0:T(8,128)(2,1)} %copy.74) | copy-start | bytes 1179652
  489.5 3.9 copy-start.15
  489.5 3.9 copy-start.32
  (19 other events, 41.7 us)
Sparse Core Ops, SparseCore 0:
  9.6 91.2 all-gather.8
  102.8 32.2 all-gather.12
  137.0 32.1 all-gather.14
  170.9 58.6 all-gather.6
  231.4 58.6 all-gather.10
  351.9 25.5 all-gather.16
  381.4 60.3 reduce-scatter.4
  445.3 109.7 reduce-scatter.6
